TPU v7x, 32 devices: a whole 2x2x4 slice. The times are simulated.
32 devices in a mesh: groups: 2 (over y), tok: 4 (over z), lay: 2 (over x), head: 2 (over core).
Axes of the slice: x: 2, y: 2, z: 4, core: 2. Of those that a mesh axis runs over, the one named last changes fastest.
Arguments:
- keys: float32 [2, 4096, 1024], P('lay', ('groups', 'tok'), 'head'), parts along dimension 1, may hold values from -80 to 80, as said below
- values: float32 [2, 4096, 1024], P('lay', ('groups', 'tok'), 'head'), parts along dimension 1, may hold values from -24 to 24
- queries: float32 [2, 32, 8192], P('lay', 'groups', 'head'), parts along dimension 1, may hold values from -620 to 620, as said below
- start_block: float32 [4096, 256], P(('groups', 'tok')), parts along dimension 0, may hold values from -6 to 6
- lengths: int32 [32], P('groups'), parts along dimension 0, may hold values from 1 to 2048, as said below
Outputs:
- attended: float32 [2, 32, 2, 4096], P('lay', 'groups', 'head', 'tok'), parts along dimension 1
There are 2 independent parts, one for each index of `groups`. A program takes and returns all parts, laid end to end along the dimension named above; each array names one. Nothing has to cross between parts.
Inputs may be any that keep to these rules, and one draw needn't show every extreme that they name: keys lie within this range. queries lie within this range. `lengths`: the longest row covers all 2048 tokens.
All inputs are finite; a program needn't handle non-finite values.
Results may differ from a plain program's by a relative error of at most 0.0003.
Values sent between devices are 32-bit elements; how exact they have to be, the bound alone decides.
No kernel may reach another device: no remote copies, remote signals or barrier semaphores. Data moves between devices by JAX's collectives and lax.ppermute only.
A program may use at most 64 MiB of HBM per device.

v0:
```python
import math
import jax
import jax.numpy as jnp
from jax import lax
from jax.sharding import PartitionSpec as P

KVH = 8
HD = 128
QH = 64
ITERS = 2
NEG = -1e30


def joined(part, axis, combine):
    gathered = jax.tree.map(lambda a: lax.all_gather(a, axis), part)

    def take(source):
        return jax.tree.map(lambda a: lax.dynamic_index_in_dim(a, source, 0, False), gathered)

    return lax.fori_loop(
        1, lax.axis_size(axis), lambda source, state: combine(state, take(source)), take(0)
    )


def gram_of(block):
    return jnp.dot(
        block.T, block, precision=lax.Precision.HIGHEST, preferred_element_type=jnp.float32
    )


def right_solve(lower, matrix):
    return lax.linalg.triangular_solve(lower, matrix, left_side=False, lower=True, transpose_a=True)


def project(keys, basis):
    return jnp.einsum("lsc,sr->lcr", keys, basis, precision=lax.Precision.HIGHEST)


def mix_block(keys, coef):
    partial_block = jnp.einsum("lsc,lcr->sr", keys, coef, precision=lax.Precision.HIGHEST)
    return lax.psum(partial_block, ("lay", "head"))


def combine(first, second):
    top = jnp.maximum(first[0], second[0])
    scale_one = jnp.exp(first[0] - top)
    scale_two = jnp.exp(second[0] - top)
    total = first[1] * scale_one + second[1] * scale_two
    summed = first[2] * scale_one[..., None] + second[2] * scale_two[..., None]
    return (top, total, summed)


def body(keys, values, queries, start_block, lengths):
    highest = lax.Precision.HIGHEST
    lay_dev, tok_dev, kv_dev = keys.shape
    rank = start_block.shape[1]
    rows = queries.shape[1]
    local_heads = queries.shape[2] // HD
    group = QH // KVH
    kv_local = kv_dev // HD

    def finish(block):
        gram, proj = lax.psum((gram_of(block), project(keys, block)), "tok")
        lower = jnp.linalg.cholesky(gram)
        coef_new = right_solve(lower, proj.reshape(-1, rank)).reshape(proj.shape)
        return (right_solve(lower, block), coef_new)

    basis, coef = finish(start_block)
    for step in range(ITERS):
        basis, coef = finish(mix_block(keys, coef))
    quer = queries.reshape(lay_dev, rows, kv_local, group, HD)
    factor = coef.reshape(lay_dev, kv_local, HD, rank)
    reduced = jnp.einsum("lbgid,lgdr->lgibr", quer, factor, precision=highest) / math.sqrt(HD)
    reduced = reduced.reshape(lay_dev, kv_local, group * rows, rank)
    scores = jnp.einsum("tr,lgxr->tlgx", basis, reduced, precision=highest)
    position = lax.axis_index("tok") * tok_dev + jnp.arange(tok_dev, dtype=jnp.int32)
    valid = position[:, None] < lengths[None, :]
    valid = jnp.tile(valid, (1, group))[:, None, None, :]
    peak = jnp.max(jnp.where(valid, scores, NEG), axis=0)
    weight = jnp.where(valid, jnp.exp(scores - peak[None]), 0.0)
    total = jnp.sum(weight, axis=0)
    vals = values.reshape(lay_dev, tok_dev, kv_local, HD)
    summed = jnp.einsum("tlgx,ltgd->lgxd", weight, vals, precision=highest)
    peak = peak.reshape(lay_dev, local_heads, rows)
    total = total.reshape(lay_dev, local_heads, rows)
    summed = summed.reshape(lay_dev, local_heads, rows, HD)
    share = local_heads // lax.axis_size("tok")
    top, whole_total, whole_sum = joined((peak, total, summed), "tok", combine)
    result = whole_sum / whole_total[..., None]
    result = lax.dynamic_slice_in_dim(result, lax.axis_index("tok") * share, share, 1)
    result = result.transpose(0, 2, 1, 3)
    return result.reshape(lay_dev, rows, 1, share * HD)


def solution(mesh):
    return jax.shard_map(
        body,
        mesh=mesh,
        in_specs=(
            P("lay", ("groups", "tok"), "head"),
            P("lay", ("groups", "tok"), "head"),
            P("lay", "groups", "head"),
            P(("groups", "tok"), None),
            P("groups"),
        ),
        out_specs=P("lay", "groups", "head", "tok"),
        check_vma=False,
    )
```

profile of v0, /device:TPU:0, one launch (start us, length us, event | category | flops | bytes accessed | tf_op | source)
XLA Modules:
  0.0 476.8 jit_solution(16566091933869575326)
XLA Ops:
  6.5 3.0 fusion.71
  9.6 2.6 fusion.9
  12.4 46.5 %all-reduce.18.cloned.1.call-done = (f32[512,256]{1,0:T(8,128)}, f32[256,256]{0,1:T(8,128)}) async-done(((f32[512,256]{1,0:T(8,128)}, f32[256,256]{0,1:T(8,128)}), (f32[512,256]{1,0:T(8,128)}, f32[256,256]{0,1:T(8,128)})) %all-reduce.18.cloned.1.call-update) | async-done | bytes 786448 | tf_op jit(solution)/shard_map/psum | solution.py:63
  59.0 1.1 copy.45
  60.2 11.7 %cholesky.172 = f32[128,128]{1,0:T(8,128)S(1)} custom-call(f32[128,128]{1,0:T(8,128)S(1)} %cholesky.270), custom_call_target="Cholesky" | custom-call | tf_op jit(solution)/shard_map/jit(cholesky)/cholesky | solution.py:64
  71.9 9.8 %custom-call.16 = f32[1,128,128]{1,2,0:T(8,128)S(1)} custom-call(f32[1,128,128]{2,1,0:T(8,128)S(1)} %get-tuple-element.288), custom_call_target="InvertDiagBlocksLowerTriangular" | custom-call | tf_op jit(solution)/shard_map/jit(cholesky)/cholesky | solution.py:64
  82.3 11.7 %cholesky.189 = f32[128,128]{1,0:T(8,128)S(1)} custom-call(f32[128,128]{1,0:T(8,128)S(1)} %convolution_subtract_fusion.6), custom_call_target="Cholesky" | custom-call | tf_op jit(solution)/shard_map/jit(cholesky)/cholesky | solution.py:64
  96.2 4.5 while.28
  97.1 1.4 bitcast_dynamic-update-slice_fusion.6
  99.2 1.4 bitcast_dynamic-update-slice_fusion.6
  100.7 19.7 %custom-call.17 = f32[2,128,128]{1,2,0:T(8,128)S(1)} custom-call(f32[2,128,128]{2,1,0:T(8,128)S(1)} %get-tuple-element.212), custom_call_target="InvertDiagBlocksLowerTriangular" | custom-call | tf_op jit(solution)/shard_map/triangular_solve/custom-call.0 | solution.py:32
  121.8 1.9 convolution_bitcast_fusion.3
  123.8 32.6 %all-reduce.10.cloned.1.call-done = f32[512,256]{0,1:T(8,128)} async-done(((f32[512,256]{0,1:T(8,128)}), f32[512,256]{0,1:T(8,128)}) %all-reduce.10.cloned.1.call-update) | async-done | bytes 524304 | tf_op jit(solution)/shard_map/psum | solution.py:41
  156.4 3.0 convolution_bitcast_fusion.2
  159.3 1.3 fusion.72
  161.1 43.7 %all-reduce.16.cloned.1.call-done = (f32[512,256]{0,1:T(8,128)}, f32[256,256]{0,1:T(8,128)}) async-done(((f32[512,256]{0,1:T(8,128)}, f32[256,256]{0,1:T(8,128)}), (f32[512,256]{0,1:T(8,128)}, f32[256,256]{0,1:T(8,128)})) %all-reduce.16.cloned.1.call-update) | async-done | bytes 786448 | tf_op jit(solution)/shard_map/psum | solution.py:63
  204.8 1.1 copy.47
  206.0 11.7 %cholesky.206 = f32[128,128]{1,0:T(8,128)S(1)} custom-call(f32[128,128]{1,0:T(8,128)S(1)} %cholesky.273), custom_call_target="Cholesky" | custom-call | tf_op jit(solution)/shard_map/jit(cholesky)/cholesky | solution.py:64
  217.8 9.8 %custom-call.18 = f32[1,128,128]{1,2,0:T(8,128)S(1)} custom-call(f32[1,128,128]{2,1,0:T(8,128)S(1)} %get-tuple-element.284), custom_call_target="InvertDiagBlocksLowerTriangular" | custom-call | tf_op jit(solution)/shard_map/jit(cholesky)/cholesky | solution.py:64
  228.1 11.7 %cholesky.223 = f32[128,128]{1,0:T(8,128)S(1)} custom-call(f32[128,128]{1,0:T(8,128)S(1)} %convolution_subtract_fusion.5), custom_call_target="Cholesky" | custom-call | tf_op jit(solution)/shard_map/jit(cholesky)/cholesky | solution.py:64
  242.6 16.1 %while.29 = (s32[]{:T(128)}, f32[256,256]{1,0:T(8,128)S(1)}, s32[2,2]{1,0:T(2,128)S(1)}, f32[2,128,128]{2,1,0:T(8,128)S(1)}, s32[]{:T(128)}) while((s32[]{:T(128)}, f32[256,256]{1,0:T(8,128)S(1)}, s32[2,2]{1,0:T(2,128)S(1)}, f32[2,128,128]{2,1,0:T(8,128)S(1)}, s32[]{:T(128)}) %tuple.129), condition=%wide.while_cond.clone, body=%wide.while_body.clone.sunk | while | flops 2 | bytes 131181 | solution.py:32
  255.1 1.4 bitcast_dynamic-update-slice_fusion.7
  257.3 1.4 bitcast_dynamic-update-slice_fusion.7
  258.7 19.7 %custom-call.19 = f32[2,128,128]{1,2,0:T(8,128)S(1)} custom-call(f32[2,128,128]{2,1,0:T(8,128)S(1)} %get-tuple-element.213), custom_call_target="InvertDiagBlocksLowerTriangular" | custom-call | tf_op jit(solution)/shard_map/triangular_solve/custom-call.0 | solution.py:32
  279.7 1.9 convolution_bitcast_fusion.1
  281.6 32.6 %all-reduce.12.cloned.1.call-done = f32[512,256]{0,1:T(8,128)} async-done(((f32[512,256]{0,1:T(8,128)}), f32[512,256]{0,1:T(8,128)}) %all-reduce.12.cloned.1.call-update) | async-done | bytes 524304 | tf_op jit(solution)/shard_map/psum | solution.py:41
  314.2 3.0 convolution_bitcast_fusion
  317.2 1.3 fusion.73
  321.1 1.6 reshape.164
  322.7 39.9 %all-reduce.14.cloned.1.call-done = (f32[512,256]{0,1:T(8,128)}, f32[256,256]{0,1:T(8,128)}) async-done(((f32[512,256]{0,1:T(8,128)}, f32[256,256]{0,1:T(8,128)}), (f32[512,256]{0,1:T(8,128)}, f32[256,256]{0,1:T(8,128)})) %all-reduce.14.cloned.1.call-update) | async-done | bytes 786448 | tf_op jit(solution)/shard_map/psum | solution.py:63
  362.6 1.1 copy.50
  363.8 11.7 %cholesky.240 = f32[128,128]{1,0:T(8,128)S(1)} custom-call(f32[128,128]{1,0:T(8,128)S(1)} %cholesky.276), custom_call_target="Cholesky" | custom-call | tf_op jit(solution)/shard_map/jit(cholesky)/cholesky | solution.py:64
  375.6 9.8 %custom-call.20 = f32[1,128,128]{1,2,0:T(8,128)S(1)} custom-call(f32[1,128,128]{2,1,0:T(8,128)S(1)} %get-tuple-element.280), custom_call_target="InvertDiagBlocksLowerTriangular" | custom-call | tf_op jit(solution)/shard_map/jit(cholesky)/cholesky | solution.py:64
  385.9 11.7 %cholesky.257 = f32[128,128]{1,0:T(8,128)S(1)} custom-call(f32[128,128]{1,0:T(8,128)S(1)} %convolution_subtract_fusion.4), custom_call_target="Cholesky" | custom-call | tf_op jit(solution)/shard_map/jit(cholesky)/cholesky | solution.py:64
  400.5 4.5 while.30
  401.3 1.4 bitcast_dynamic-update-slice_fusion.8
  403.5 1.4 bitcast_dynamic-update-slice_fusion.8
  404.9 19.7 %custom-call.21 = f32[2,128,128]{1,2,0:T(8,128)S(1)} custom-call(f32[2,128,128]{2,1,0:T(8,128)S(1)} %get-tuple-element.214), custom_call_target="InvertDiagBlocksLowerTriangular" | custom-call | tf_op jit(solution)/shard_map/triangular_solve/custom-call.0 | solution.py:32
  426.6 1.1 fusion.61
  429.2 1.7 convolution_multiply_fusion
  430.9 1.9 select_reduce_fusion
  432.8 2.6 fusion.11
  436.0 13.2 %all_gather.10 = f32[4,1,32,16]{2,3,1,0:T(8,128)S(1)} all-gather(f32[1,1,32,16]{2,3,1,0:T(8,128)S(1)} %copy.57), channel_id=1, replica_groups=mesh['groups'=2,'tok'=4,'lay'=2,'head'=2] {'tok'}, dimensions={0}, use_global_device_ids=true | all-gather | bytes 10240 | tf_op jit(solution)/shard_map/all_gather | solution.py:15
  449.2 13.3 %all_gather.9 = f32[4,1,32,16]{2,3,1,0:T(8,128)S(1)} all-gather(f32[1,1,32,16]{2,3,1,0:T(8,128)S(1)} %copy.56), channel_id=1, replica_groups=mesh['groups'=2,'tok'=4,'lay'=2,'head'=2] {'tok'}, dimensions={0}, use_global_device_ids=true | all-gather | bytes 10240 | tf_op jit(solution)/shard_map/all_gather | solution.py:15
  464.5 4.3 while.27
  464.7 1.2 fusion.107
  466.2 1.2 fusion.107
  467.6 1.2 fusion.107
  (138 shorter events, 22.8 us)
Async XLA Ops:
  6.5 3.0 copy-start
  6.5 3.0 copy-start.2
  6.5 52.4 %all-reduce.18.cloned.1.call-start = ((), (), s32[]{:S(2)}) async-start(), calls=%async_computation.5 | async-start | bytes 1572864 | tf_op jit(solution)/shard_map/psum | solution.py:63
  12.2 144.2 %all-reduce.10.cloned.1.call-start = ((), (), s32[]{:S(2)}) async-start(), calls=%async_computation | async-start | bytes 1048576 | tf_op jit(solution)/shard_map/psum | solution.py:41
  59.0 1.2 copy-start.6
  96.1 24.3 %copy-start.13 = (f32[512,256]{1,0:T(8,128)S(1)}, f32[512,256]{1,0:T(8,128)}, u32[]{:S(2)}) copy-start(f32[512,256]{1,0:T(8,128)} %get-tuple-element.265) | copy-start | bytes 1572868
  123.7 81.1 %all-reduce.16.cloned.1.call-start = ((), (), s32[]{:S(2)}) async-start(), calls=%async_computation.4 | async-start | bytes 1572864 | tf_op jit(solution)/shard_map/psum | solution.py:63
  156.4 3.0 copy-start.3
  160.7 153.5 %all-reduce.12.cloned.1.call-start = ((), (), s32[]{:S(2)}) async-start(), calls=%async_computation.1 | async-start | bytes 1048576 | tf_op jit(solution)/shard_map/psum | solution.py:41
  204.8 1.2 copy-start.7
  242.6 35.8 %copy-start.14 = (f32[512,256]{0,1:T(8,128)S(1)}, f32[512,256]{0,1:T(8,128)}, u32[]{:S(2)}) copy-start(f32[512,256]{0,1:T(8,128)} %get-tuple-element.263) | copy-start | bytes 1572868
  281.5 81.0 %all-reduce.14.cloned.1.call-start = ((), (), s32[]{:S(2)}) async-start(), calls=%async_computation.3 | async-start | bytes 1572864 | tf_op jit(solution)/shard_map/psum | solution.py:63
  314.2 3.0 copy-start.1
  318.5 0.9 copy-start.15
  318.5 145.0 %all-gather.2.cloned.1.call-start = ((), (), s32[]{:S(2)}) async-start(), calls=%async_computation.2 | async-start | bytes 1310720 | tf_op jit(solution)/shard_map/all_gather | solution.py:15
  320.2 0.7 copy-start.16
  362.6 1.2 copy-start.4
  363.8 11.7 %copy-start.8 = (f32[256,256]{1,0:T(8,128)}, f32[256,256]{1,0:T(8,128)S(1)}, u32[]{:S(2)}) copy-start(f32[256,256]{1,0:T(8,128)S(1)} %fusion.34) | copy-start | bytes 786436
  375.6 9.8 %copy-start.9 = (f32[256,256]{1,0:T(8,128)S(1)}, f32[256,256]{1,0:T(8,128)}, u32[]{:S(2)}) copy-start(f32[256,256]{1,0:T(8,128)} %copy-done.8) | copy-start | bytes 786436
  424.6 0.6 copy-start.10
  425.7 0.9 copy-start.11
  425.7 2.0 copy-start.12
  429.2 1.7 copy-start.5
Sparse Core Ops, SparseCore 0:
  12.3 46.5 all-reduce.17
  123.8 32.5 all-reduce.9
  160.8 43.8 all-reduce.15
  281.7 32.4 all-reduce.11
  318.6 43.8 all-reduce.13
  435.6 27.8 all-gather.1
where the time goes:
time: 480 us; the launch traced here: 477 us
  waiting for transfers between devices  196 us (41%)
  other arithmetic  167 us (35%)
  matrix products  31.4 us (7%)
  blocking collectives  26.5 us (6%)
  local copies, waits for them, and re-layouts  24 us (5%)
  between operations  18.3 us (4%)
  loops' own time  12.5 us (3%)
    psum x3, waiting for transfers between devices, finish(): gram, proj = lax.psum((gram_of(block), project(keys, block)), 'tok')  130 us
    another operation x20, other arithmetic, finish(): lower = jnp.linalg.cholesky(gram)  103 us
    psum x2, waiting for transfers between devices, mix_block(): return lax.psum(partial_block, ('lay', 'head'))  65.2 us
    another operation x8, other arithmetic, right_solve(): lax.linalg.triangular_solve(lower, matrix, left_side=False, lower=True, t...  59.2 us
    all_gather x2, blocking collectives, joined(): gathered = jax.tree.map(lambda a: lax.all_gather(a, axis), part)  26.5 us
    another operation x22, local copies, waits for them, and re-layouts, right_solve(): lax.linalg.triangular_solve(lower, matrix, left_side=False, lower=True, t...  12.7 us
    another operation x3, loops' own time, right_solve(): lax.linalg.triangular_solve(lower, matrix, left_side=False, lower=True, t...  12.4 us
  transfers between devices with their start and end apart: 6, of which 6 were waited for; matrix products, arithmetic and copies ran while one was open for 1% of the time, Pallas kernels for 0%

commit v1 on v0

--- a/solution.py
+++ b/solution.py
@@ -38,7 +38,7 @@
 
 def mix_block(keys, coef):
     partial_block = jnp.einsum("lsc,lcr->sr", keys, coef, precision=lax.Precision.HIGHEST)
-    return lax.psum(partial_block, ("lay", "head"))
+    return lax.psum(lax.psum(partial_block, "head"), "lay")
 
 
 def combine(first, second):

time: 480 us -> 516 us (1.075)
  waiting for transfers between devices: 196 us -> 232 us
    psum x2 -> x4, waiting for transfers between devices: 65.2 us -> 100 us  [mix_block(): return lax.psum(lax.psum(partial_block, 'head'), 'lay')]
  transfers between devices with their start and end apart: 6 -> 8, of which waited for: 6 -> 8; matrix products, arithmetic and copies ran while one was open for 1% -> 1% of each run, Pallas kernels for 0% -> 0%
where the time goes in v1:
time: 516 us; the launch traced here: 512 us
  waiting for transfers between devices  232 us (45%)
  other arithmetic  167 us (32%)
  matrix products  31.4 us (6%)
  blocking collectives  26.5 us (5%)
  local copies, waits for them, and re-layouts  24 us (5%)
  between operations  18.3 us (4%)
  loops' own time  12.6 us (2%)
    psum x3, waiting for transfers between devices, finish(): gram, proj = lax.psum((gram_of(block), project(keys, block)), 'tok')  130 us
    another operation x20, other arithmetic, finish(): lower = jnp.linalg.cholesky(gram)  103 us
    psum x4, waiting for transfers between devices, mix_block(): return lax.psum(lax.psum(partial_block, 'head'), 'lay')  100 us
    another operation x8, other arithmetic, right_solve(): lax.linalg.triangular_solve(lower, matrix, left_side=False, lower=True, t...  59.2 us
    all_gather x2, blocking collectives, joined(): gathered = jax.tree.map(lambda a: lax.all_gather(a, axis), part)  26.5 us
    another operation x22, local copies, waits for them, and re-layouts, right_solve(): lax.linalg.triangular_solve(lower, matrix, left_side=False, lower=True, t...  12.7 us
    another operation x3, loops' own time, right_solve(): lax.linalg.triangular_solve(lower, matrix, left_side=False, lower=True, t...  12.4 us
  transfers between devices with their start and end apart: 8, of which 8 were waited for; matrix products, arithmetic and copies ran while one was open for 1% of the time, Pallas kernels for 0%

profile of v1, /device:TPU:0, one launch (start us, length us, event | category | flops | bytes accessed | tf_op | source)
XLA Modules:
  0.0 512.1 jit_solution(1451805544435260492)
XLA Ops:
  6.5 3.0 fusion.71
  9.6 2.6 fusion.9
  12.4 46.5 %all-reduce.24.cloned.1.call-done = (f32[512,256]{1,0:T(8,128)}, f32[256,256]{0,1:T(8,128)}) async-done(((f32[512,256]{1,0:T(8,128)}, f32[256,256]{0,1:T(8,128)}), (f32[512,256]{1,0:T(8,128)}, f32[256,256]{0,1:T(8,128)})) %all-reduce.24.cloned.1.call-update) | async-done | bytes 786448 | tf_op jit(solution)/shard_map/psum | solution.py:63
  59.0 1.1 copy.45
  60.2 11.7 %cholesky.172 = f32[128,128]{1,0:T(8,128)S(1)} custom-call(f32[128,128]{1,0:T(8,128)S(1)} %cholesky.270), custom_call_target="Cholesky" | custom-call | tf_op jit(solution)/shard_map/jit(cholesky)/cholesky | solution.py:64
  71.9 9.8 %custom-call.16 = f32[1,128,128]{1,2,0:T(8,128)S(1)} custom-call(f32[1,128,128]{2,1,0:T(8,128)S(1)} %get-tuple-element.288), custom_call_target="InvertDiagBlocksLowerTriangular" | custom-call | tf_op jit(solution)/shard_map/jit(cholesky)/cholesky | solution.py:64
  82.3 11.7 %cholesky.189 = f32[128,128]{1,0:T(8,128)S(1)} custom-call(f32[128,128]{1,0:T(8,128)S(1)} %convolution_subtract_fusion.6), custom_call_target="Cholesky" | custom-call | tf_op jit(solution)/shard_map/jit(cholesky)/cholesky | solution.py:64
  96.2 4.5 while.28
  97.1 1.4 bitcast_dynamic-update-slice_fusion.6
  99.2 1.4 bitcast_dynamic-update-slice_fusion.6
  100.7 19.7 %custom-call.17 = f32[2,128,128]{1,2,0:T(8,128)S(1)} custom-call(f32[2,128,128]{2,1,0:T(8,128)S(1)} %get-tuple-element.212), custom_call_target="InvertDiagBlocksLowerTriangular" | custom-call | tf_op jit(solution)/shard_map/triangular_solve/custom-call.0 | solution.py:32
  121.8 1.9 convolution_bitcast_fusion.3
  123.8 18.2 %all-reduce.12.cloned.1.call-done = f32[512,256]{0,1:T(8,128)} async-done(((f32[512,256]{0,1:T(8,128)}), f32[512,256]{0,1:T(8,128)}) %all-reduce.12.cloned.1.call-update) | async-done | bytes 524304 | tf_op jit(solution)/shard_map/psum | solution.py:41
  142.0 32.1 %all-reduce.14.cloned.1.call-done = f32[512,256]{0,1:T(8,128)} async-done(((f32[512,256]{0,1:T(8,128)}), f32[512,256]{0,1:T(8,128)}) %all-reduce.14.cloned.1.call-update) | async-done | bytes 524304 | tf_op jit(solution)/shard_map/psum | solution.py:41
  174.1 3.0 convolution_bitcast_fusion.2
  177.1 1.3 fusion.72
  178.8 43.7 %all-reduce.22.cloned.1.call-done = (f32[512,256]{0,1:T(8,128)}, f32[256,256]{0,1:T(8,128)}) async-done(((f32[512,256]{0,1:T(8,128)}, f32[256,256]{0,1:T(8,128)}), (f32[512,256]{0,1:T(8,128)}, f32[256,256]{0,1:T(8,128)})) %all-reduce.22.cloned.1.call-update) | async-done | bytes 786448 | tf_op jit(solution)/shard_map/psum | solution.py:63
  222.5 1.1 copy.47
  223.7 11.7 %cholesky.206 = f32[128,128]{1,0:T(8,128)S(1)} custom-call(f32[128,128]{1,0:T(8,128)S(1)} %cholesky.273), custom_call_target="Cholesky" | custom-call | tf_op jit(solution)/shard_map/jit(cholesky)/cholesky | solution.py:64
  235.5 9.8 %custom-call.18 = f32[1,128,128]{1,2,0:T(8,128)S(1)} custom-call(f32[1,128,128]{2,1,0:T(8,128)S(1)} %get-tuple-element.284), custom_call_target="InvertDiagBlocksLowerTriangular" | custom-call | tf_op jit(solution)/shard_map/jit(cholesky)/cholesky | solution.py:64
  245.8 11.7 %cholesky.223 = f32[128,128]{1,0:T(8,128)S(1)} custom-call(f32[128,128]{1,0:T(8,128)S(1)} %convolution_subtract_fusion.5), custom_call_target="Cholesky" | custom-call | tf_op jit(solution)/shard_map/jit(cholesky)/cholesky | solution.py:64
  260.4 16.1 %while.29 = (s32[]{:T(128)}, f32[256,256]{1,0:T(8,128)S(1)}, s32[2,2]{1,0:T(2,128)S(1)}, f32[2,128,128]{2,1,0:T(8,128)S(1)}, s32[]{:T(128)}) while((s32[]{:T(128)}, f32[256,256]{1,0:T(8,128)S(1)}, s32[2,2]{1,0:T(2,128)S(1)}, f32[2,128,128]{2,1,0:T(8,128)S(1)}, s32[]{:T(128)}) %tuple.133), condition=%wide.while_cond.clone, body=%wide.while_body.clone.sunk | while | flops 2 | bytes 131181 | solution.py:32
  272.9 1.4 bitcast_dynamic-update-slice_fusion.7
  275.0 1.4 bitcast_dynamic-update-slice_fusion.7
  276.5 19.7 %custom-call.19 = f32[2,128,128]{1,2,0:T(8,128)S(1)} custom-call(f32[2,128,128]{2,1,0:T(8,128)S(1)} %get-tuple-element.213), custom_call_target="InvertDiagBlocksLowerTriangular" | custom-call | tf_op jit(solution)/shard_map/triangular_solve/custom-call.0 | solution.py:32
  297.4 1.9 convolution_bitcast_fusion.1
  299.4 18.2 %all-reduce.16.cloned.1.call-done = f32[512,256]{0,1:T(8,128)} async-done(((f32[512,256]{0,1:T(8,128)}), f32[512,256]{0,1:T(8,128)}) %all-reduce.16.cloned.1.call-update) | async-done | bytes 524304 | tf_op jit(solution)/shard_map/psum | solution.py:41
  317.6 32.0 %all-reduce.18.cloned.1.call-done = f32[512,256]{0,1:T(8,128)} async-done(((f32[512,256]{0,1:T(8,128)}), f32[512,256]{0,1:T(8,128)}) %all-reduce.18.cloned.1.call-update) | async-done | bytes 524304 | tf_op jit(solution)/shard_map/psum | solution.py:41
  349.6 3.0 convolution_bitcast_fusion
  352.5 1.3 fusion.73
  356.5 1.6 reshape.164
  358.0 39.9 %all-reduce.20.cloned.1.call-done = (f32[512,256]{0,1:T(8,128)}, f32[256,256]{0,1:T(8,128)}) async-done(((f32[512,256]{0,1:T(8,128)}, f32[256,256]{0,1:T(8,128)}), (f32[512,256]{0,1:T(8,128)}, f32[256,256]{0,1:T(8,128)})) %all-reduce.20.cloned.1.call-update) | async-done | bytes 786448 | tf_op jit(solution)/shard_map/psum | solution.py:63
  399.2 11.7 %cholesky.240 = f32[128,128]{1,0:T(8,128)S(1)} custom-call(f32[128,128]{1,0:T(8,128)S(1)} %cholesky.276), custom_call_target="Cholesky" | custom-call | tf_op jit(solution)/shard_map/jit(cholesky)/cholesky | solution.py:64
  411.0 9.8 %custom-call.20 = f32[1,128,128]{1,2,0:T(8,128)S(1)} custom-call(f32[1,128,128]{2,1,0:T(8,128)S(1)} %get-tuple-element.280), custom_call_target="InvertDiagBlocksLowerTriangular" | custom-call | tf_op jit(solution)/shard_map/jit(cholesky)/cholesky | solution.py:64
  421.3 11.7 %cholesky.257 = f32[128,128]{1,0:T(8,128)S(1)} custom-call(f32[128,128]{1,0:T(8,128)S(1)} %convolution_subtract_fusion.4), custom_call_target="Cholesky" | custom-call | tf_op jit(solution)/shard_map/jit(cholesky)/cholesky | solution.py:64
  435.8 4.5 while.30
  436.7 1.4 bitcast_dynamic-update-slice_fusion.8
  438.8 1.4 bitcast_dynamic-update-slice_fusion.8
  440.3 19.7 %custom-call.21 = f32[2,128,128]{1,2,0:T(8,128)S(1)} custom-call(f32[2,128,128]{2,1,0:T(8,128)S(1)} %get-tuple-element.214), custom_call_target="InvertDiagBlocksLowerTriangular" | custom-call | tf_op jit(solution)/shard_map/triangular_solve/custom-call.0 | solution.py:32
  464.6 1.7 convolution_multiply_fusion
  466.3 1.9 select_reduce_fusion
  468.2 2.6 fusion.11
  471.4 13.2 %all_gather.10 = f32[4,1,32,16]{2,3,1,0:T(8,128)S(1)} all-gather(f32[1,1,32,16]{2,3,1,0:T(8,128)S(1)} %copy.57), channel_id=1, replica_groups=mesh['groups'=2,'tok'=4,'lay'=2,'head'=2] {'tok'}, dimensions={0}, use_global_device_ids=true | all-gather | bytes 10240 | tf_op jit(solution)/shard_map/all_gather | solution.py:15
  484.5 13.3 %all_gather.9 = f32[4,1,32,16]{2,3,1,0:T(8,128)S(1)} all-gather(f32[1,1,32,16]{2,3,1,0:T(8,128)S(1)} %copy.56), channel_id=1, replica_groups=mesh['groups'=2,'tok'=4,'lay'=2,'head'=2] {'tok'}, dimensions={0}, use_global_device_ids=true | all-gather | bytes 10240 | tf_op jit(solution)/shard_map/all_gather | solution.py:15
  499.9 4.3 while.27
  500.1 1.2 fusion.107
  501.5 1.2 fusion.107
  503.0 1.2 fusion.107
  (144 shorter events, 25.1 us)
Async XLA Ops:
  6.5 3.0 copy-start
  6.5 3.0 copy-start.2
  6.5 52.4 %all-reduce.24.cloned.1.call-start = ((), (), s32[]{:S(2)}) async-start(), calls=%async_computation.7 | async-start | bytes 1572864 | tf_op jit(solution)/shard_map/psum | solution.py:63
  12.2 129.7 %all-reduce.12.cloned.1.call-start = ((), (), s32[]{:S(2)}) async-start(), calls=%async_computation | async-start | bytes 1048576 | tf_op jit(solution)/shard_map/psum | solution.py:41
  59.0 1.2 copy-start.6
  96.1 24.3 %copy-start.13 = (f32[512,256]{1,0:T(8,128)S(1)}, f32[512,256]{1,0:T(8,128)}, u32[]{:S(2)}) copy-start(f32[512,256]{1,0:T(8,128)} %get-tuple-element.265) | copy-start | bytes 1572868
  123.7 50.4 %all-reduce.14.cloned.1.call-start = ((), (), s32[]{:S(2)}) async-start(), calls=%async_computation.1 | async-start | bytes 1048576 | tf_op jit(solution)/shard_map/psum | solution.py:41
  141.9 80.6 %all-reduce.22.cloned.1.call-start = ((), (), s32[]{:S(2)}) async-start(), calls=%async_computation.6 | async-start | bytes 1572864 | tf_op jit(solution)/shard_map/psum | solution.py:63
  174.1 3.0 copy-start.3
  178.4 139.1 %all-reduce.16.cloned.1.call-start = ((), (), s32[]{:S(2)}) async-start(), calls=%async_computation.2 | async-start | bytes 1048576 | tf_op jit(solution)/shard_map/psum | solution.py:41
  222.5 1.2 copy-start.7
  260.3 35.9 %copy-start.14 = (f32[512,256]{0,1:T(8,128)S(1)}, f32[512,256]{0,1:T(8,128)}, u32[]{:S(2)}) copy-start(f32[512,256]{0,1:T(8,128)} %get-tuple-element.263) | copy-start | bytes 1572868
  299.3 50.3 %all-reduce.18.cloned.1.call-start = ((), (), s32[]{:S(2)}) async-start(), calls=%async_computation.3 | async-start | bytes 1048576 | tf_op jit(solution)/shard_map/psum | solution.py:41
  317.5 80.4 %all-reduce.20.cloned.1.call-start = ((), (), s32[]{:S(2)}) async-start(), calls=%async_computation.5 | async-start | bytes 1572864 | tf_op jit(solution)/shard_map/psum | solution.py:63
  349.6 3.0 copy-start.1
  353.8 0.9 copy-start.15
  353.9 145.0 %all-gather.2.cloned.1.call-start = ((), (), s32[]{:S(2)}) async-start(), calls=%async_computation.4 | async-start | bytes 1310720 | tf_op jit(solution)/shard_map/all_gather | solution.py:15
  355.5 0.7 copy-start.16
  397.9 1.2 copy-start.4
  399.1 11.7 %copy-start.8 = (f32[256,256]{1,0:T(8,128)}, f32[256,256]{1,0:T(8,128)S(1)}, u32[]{:S(2)}) copy-start(f32[256,256]{1,0:T(8,128)S(1)} %fusion.34) | copy-start | bytes 786436
  410.9 9.8 %copy-start.9 = (f32[256,256]{1,0:T(8,128)S(1)}, f32[256,256]{1,0:T(8,128)}, u32[]{:S(2)}) copy-start(f32[256,256]{1,0:T(8,128)} %copy-done.8) | copy-start | bytes 786436
  460.0 0.6 copy-start.10
  461.1 0.9 copy-start.11
  461.1 2.0 copy-start.12
  464.6 1.7 copy-start.5
Sparse Core Ops, SparseCore 0:
  12.3 46.5 all-reduce.23
  123.8 18.0 all-reduce.11
  144.3 29.7 all-reduce.13
  178.5 43.8 all-reduce.21
  299.4 18.0 all-reduce.15
  319.8 29.7 all-reduce.17
  354.0 43.8 all-reduce.19
  471.0 27.8 all-gather.1
